TPU v7x, 512 devices: a whole 4x4x16 slice. The times are simulated.
512 devices in a mesh: grp: 16 (over y, x_hi, core), seq: 32 (over z, x_lo).
Axes of the slice: x: 4 (x_hi: 2, x_lo: 2; x = x_hi * 2 + x_lo), y: 4, z: 16, core: 2. Of those that a mesh axis runs over, the one named last changes fastest.
Arguments:
- tokens: bfloat16 [16, 4096, 1024], P('grp', 'seq'), may hold values from -40 to 40
- queries: bfloat16 [16, 4096, 512], P('grp', 'seq'), may hold values from -8 to 8
- keys: bfloat16 [16, 4096, 512], P('grp', 'seq'), may hold values from -8 to 8
- values: bfloat16 [16, 4096, 512], P('grp', 'seq'), may hold values from -6 to 6
- attn_mask: int32 [16, 32, 32], P('grp', 'seq'), may hold values from 0 to 1, as said below
- out_proj: bfloat16 [512, 1024], replicated, may hold values from -0.25 to 0.25
- norm_gain_vector: float32 [1024], replicated, may hold values from 0.5 to 1.5
- w1_packed: bfloat16 [32, 2, 128, 128], P('grp'), may hold values from -0.375 to 0.375
- w1_rows: int32 [32, 2], replicated, may hold values from 0 to 7, as said below
- w2_packed: bfloat16 [32, 2, 128, 128], P('grp'), may hold values from -0.1875 to 0.1875
- w2_cols: int32 [32, 2], replicated, may hold values from 0 to 7, as said below
- grad_out: bfloat16 [16, 4096, 1024], P('grp', 'seq'), may hold values from -6 to 6
Outputs:
- output: bfloat16 [16, 4096, 1024], P('grp', 'seq')
- grad_tokens: bfloat16 [16, 4096, 1024], P('grp', 'seq')
Inputs may be any that keep to these rules, and one draw needn't show every extreme that they name: attn_mask[s, i, i] is 1 for every sheet s and block i. `w1_rows`: the 2 entries of a row are distinct. `w2_cols`: the 2 entries of a row are distinct.
All inputs are finite; a program needn't handle non-finite values.
Results may differ from a plain program's by a relative error of at most 0.0035.
The roundings to bfloat16 on the way count: a program that leaves them out, or rounds other values in their place, can miss the bound.
Values may be sent and summed in bfloat16 or wider, within the bound.
A program may use at most 64 MiB of HBM per device.

v0:
```python
import jax
import jax.numpy as jnp
from jax import lax
from jax.sharding import PartitionSpec as P

D = 1024
HD = 64
HEADS = 8
BLK = 128


def gelu_slope(pre):
    return (
        0.5 * (1.0 + jax.scipy.special.erf(pre * 0.7071067811865476))
        + pre * jnp.exp(-0.5 * pre * pre) * 0.3989422804014327
    )


def expand_mask(mask):
    rows_blk, cols_blk = mask.shape
    wide = jnp.broadcast_to(mask[:, None, :, None], (rows_blk, BLK, cols_blk, BLK))
    return wide.reshape(rows_blk * BLK, cols_blk * BLK) > 0


def split_heads(array):
    return array.reshape(array.shape[0], HEADS, HD).transpose(1, 0, 2)


def join_heads(array):
    return array.transpose(1, 0, 2).reshape(array.shape[1], HEADS * HD)


def attend_forward(query, key_rows, value_rows, allowed):
    scale = HD ** (-0.5)

    def one_head(args):
        q_head, k_head, v_head = args
        scores = jnp.dot(q_head, k_head.T, preferred_element_type=jnp.float32) * scale
        scores = jnp.where(allowed, scores, -jnp.inf)
        top = jnp.max(scores, axis=1, keepdims=True)
        weight = jnp.exp(scores - top)
        total = jnp.sum(weight, axis=1, keepdims=True)
        prob = (weight / total).astype(jnp.bfloat16)
        return jnp.dot(prob, v_head, preferred_element_type=jnp.float32)

    heads_out = lax.map(
        one_head, (split_heads(query), split_heads(key_rows), split_heads(value_rows))
    )
    return join_heads(heads_out).astype(jnp.bfloat16)


def layer_norm_forward(hidden_state, gain_vector):
    mean_row = jnp.mean(hidden_state, axis=1, keepdims=True)
    mean_removed = hidden_state - mean_row
    reciprocal_deviation = lax.rsqrt(
        jnp.mean(mean_removed * mean_removed, axis=1, keepdims=True) + 1e-06
    )
    unit_rows = mean_removed * reciprocal_deviation
    return (unit_rows, reciprocal_deviation, (unit_rows * gain_vector).astype(jnp.bfloat16))


def layer_norm_backward(
    normed_gradient, gain_vector, unit_rows, reciprocal_deviation, gradient_rows
):
    unit_gradient = normed_gradient * gain_vector
    inner_product = (
        unit_gradient
        - jnp.mean(unit_gradient, axis=1, keepdims=True)
        - unit_rows * jnp.mean(unit_gradient * unit_rows, axis=1, keepdims=True)
    )
    return (gradient_rows.astype(jnp.float32) + reciprocal_deviation * inner_product).astype(
        jnp.bfloat16
    )


def panel_terms(first_blocks, second_blocks, row_table, col_table, normed_rows, gradient_rows):
    tok_rows = normed_rows.shape[0]
    width_blocks = D // BLK
    block_ids = jnp.arange(width_blocks, dtype=jnp.int32)[None, None, :]
    row_place = (row_table[:, :, None] == block_ids).astype(jnp.float32)
    col_place = (col_table[:, :, None] == block_ids).astype(jnp.float32)
    normed_sel = jnp.take(normed_rows.reshape(tok_rows, width_blocks, BLK), row_table, axis=1)
    pre = jnp.einsum("tcnk,cnkj->tcj", normed_sel, first_blocks, preferred_element_type=jnp.float32)
    act = jax.nn.gelu(pre, approximate=False).astype(jnp.bfloat16)
    forward_part = jnp.einsum(
        "tck,cnkj->tcnj", act, second_blocks, preferred_element_type=jnp.float32
    )
    mlp_part = jnp.einsum(
        "tcnj,cnb->tbj", forward_part, col_place, precision=lax.Precision.HIGHEST
    ).reshape(tok_rows, D)
    grad_sel = jnp.take(gradient_rows.reshape(tok_rows, width_blocks, BLK), col_table, axis=1)
    dact = jnp.einsum("tcnj,cnkj->tck", grad_sel, second_blocks, preferred_element_type=jnp.float32)
    dpre = (dact * gelu_slope(pre)).astype(jnp.bfloat16)
    back_part = jnp.einsum("tcj,cnkj->tcnk", dpre, first_blocks, preferred_element_type=jnp.float32)
    dnormed_part = jnp.einsum(
        "tcnk,cnb->tbk", back_part, row_place, precision=lax.Precision.HIGHEST
    ).reshape(tok_rows, D)
    return (mlp_part, dnormed_part)


def body(
    tokens,
    queries,
    keys,
    values,
    attn_mask,
    out_proj,
    norm_gain_vector,
    w1_packed,
    w1_rows,
    w2_packed,
    w2_cols,
    grad_out,
):
    rows_in = tokens[0]
    query = queries[0]
    gradient_rows = grad_out[0]
    allowed = expand_mask(attn_mask[0])
    key_rows, value_rows = (
        lax.all_gather(keys[0], "seq", axis=0, tiled=True),
        lax.all_gather(values[0], "seq", axis=0, tiled=True),
    )
    attn = attend_forward(query, key_rows, value_rows, allowed)
    hidden_state = rows_in.astype(jnp.float32) + jnp.dot(
        attn, out_proj, preferred_element_type=jnp.float32
    )
    unit_rows, reciprocal_deviation, normed_rows = layer_norm_forward(
        hidden_state, norm_gain_vector
    )
    first_all, second_all = (
        lax.all_gather(w1_packed, "grp", axis=0, tiled=True),
        lax.all_gather(w2_packed, "grp", axis=0, tiled=True),
    )
    mlp, normed_gradient = panel_terms(
        first_all, second_all, w1_rows, w2_cols, normed_rows, gradient_rows
    )
    result = (hidden_state + mlp).astype(jnp.bfloat16)
    incoming_gradient_rows = layer_norm_backward(
        normed_gradient, norm_gain_vector, unit_rows, reciprocal_deviation, gradient_rows
    )
    return (result[None], incoming_gradient_rows[None])


def solution(mesh):
    return jax.shard_map(
        body,
        mesh=mesh,
        in_specs=(
            P("grp", "seq", None),
            P("grp", "seq", None),
            P("grp", "seq", None),
            P("grp", "seq", None),
            P("grp", "seq", None),
            P(),
            P(),
            P("grp", None, None, None),
            P(),
            P("grp", None, None, None),
            P(),
            P("grp", "seq", None),
        ),
        out_specs=(P("grp", "seq", None), P("grp", "seq", None)),
        check_vma=False,
    )
```

profile of v0, /device:TPU:1, one launch (start us, length us, event | category | flops | bytes accessed | tf_op | source)
XLA Modules:
  0.0 497.4 jit_solution(4746874300129246282)
XLA Ops:
  7.2 1.7 copy.46
  9.0 1.7 copy.47
  10.8 0.7 all-gather.7.cloned.1.call-update
  11.5 0.5 all-gather.9.cloned.1.call-update
  12.1 0.7 compare_select_fusion.1
  12.7 0.7 compare_and_fusion.1
  13.4 0.7 compare_select_fusion
  14.1 0.7 compare_and_fusion
  14.8 1.0 copy.45
  15.8 0.7 compare_bitcast_fusion
  16.9 1.1 copy.56
  18.5 2.1 gather_fusion.1
  20.6 133.6 %all-gather.11.cloned.1.call-done = bf16[1,4096,512]{1,2,0:T(8,128)(2,1)} async-done(((bf16[1,128,512]{1,2,0:T(8,128)(2,1)}), bf16[1,4096,512]{1,2,0:T(8,128)(2,1)}) %all-gather.11.cloned.1.call-update) | async-done | bytes 4194320 | tf_op jit(solution)/shard_map/all_gather | solution.py:120
  154.2 160.8 %all-gather.13.cloned.1.call-done = bf16[1,4096,512]{1,2,0:T(8,128)(2,1)} async-done(((bf16[1,128,512]{1,2,0:T(8,128)(2,1)}), bf16[1,4096,512]{1,2,0:T(8,128)(2,1)}) %all-gather.13.cloned.1.call-update) | async-done | bytes 4194320 | tf_op jit(solution)/shard_map/all_gather | solution.py:121
  315.1 29.5 %while.11 = (s32[]{:T(128)}, bf16[8,128,64]{1,2,0:T(8,128)(2,1)S(1)}, bf16[8,128,64]{1,2,0:T(8,128)(2,1)S(1)}, bf16[8,4096,64]{1,2,0:T(8,128)(2,1)}, bf16[8,4096...) while((s32[]{:T(128)}, bf16[8,128,64]{1,2,0:T(8,128)(2,1)S(1)}, ...), condition=%wide.region_3.4_spmd.clone, body=%wide.region_0.3_spmd.clone.sunk | while | flops 138411776 | bytes 7397965 | solution.py:46
  315.1 1.6 fusion.158
  316.7 0.4 fusion.159
  317.1 1.6 fusion.160
  318.8 1.6 fusion.158
  320.4 0.4 fusion.159
  320.8 1.6 fusion.160
  322.5 1.6 fusion.158
  324.0 0.4 fusion.159
  324.5 1.6 fusion.160
  326.1 1.6 fusion.158
  327.7 0.4 fusion.159
  328.2 1.6 fusion.160
  329.8 1.6 fusion.158
  331.4 0.4 fusion.159
  331.9 1.6 fusion.160
  333.5 1.6 fusion.158
  335.1 0.4 fusion.159
  335.5 1.6 fusion.160
  337.2 1.6 fusion.158
  338.8 0.4 fusion.159
  339.2 1.6 fusion.160
  340.9 1.6 fusion.158
  342.4 0.4 fusion.159
  342.9 1.6 fusion.160
  345.4 2.2 gather_fusion
  347.6 54.0 %all-gather.7.cloned.1.call-done = bf16[32,2,128,128]{3,2,1,0:T(8,128)(2,1)} async-done(((bf16[2,2,128,128]{3,2,1,0:T(8,128)(2,1)}), bf16[32,2,128,128]{3,2,1,0:T(8,128)(2,1)}) %all-gather.7.cloned.1.call-update) | async-done | bytes 2097168 | tf_op jit(solution)/shard_map/all_gather | solution.py:131
  401.6 4.3 fusion.32
  405.9 60.7 %all-gather.9.cloned.1.call-done = bf16[32,2,128,128]{3,2,1,0:T(8,128)(2,1)} async-done(((bf16[2,2,128,128]{3,2,1,0:T(8,128)(2,1)}), bf16[32,2,128,128]{3,2,1,0:T(8,128)(2,1)}) %all-gather.9.cloned.1.call-update) | async-done | bytes 2097168 | tf_op jit(solution)/shard_map/all_gather | solution.py:132
  466.6 7.2 %convolution_bitcast_fusion.1 = f32[128,32,2,128]{3,0,2,1:T(8,128)} fusion(bf16[32,2,128,128]{3,2,1,0:T(8,128)(2,1)} %all-gather.7.cloned.1.call-done, f32[32,128,128,1]{2,1,3,0:T(8,128)} %fusion.32, bf16[32,2,128,128]{3,2,1,0:T(8,128)(2,1)} %all-gather.9.cloned.1.call-done, bf16[32,2,128,128]{3,2,1,0:T(8,128)(2,1)} %bitcast.202, pred[32,2]{1,0:T(8,128)(4,1)S(1)} %copy.55), kind=kOutput, calls=%fused_computation.24 | convolution fusion | flops 543162368 | bytes 12582976 | tf_op jit(solution)/shard_map/tcj,cnkj->tcnk/dot_general | solution.py:94
  473.8 6.7 %fusion.96 = (f32[128]{0:T(128)S(1)}, f32[8,128,128,1]{2,0,3,1:T(8,128)S(1)}) fusion(f32[8,128]{1,0:T(8,128)S(1)} %bitcast.208, f32[128,32,2,128]{3,0,2,1:T(8,128)} %convolution_bitcast_fusion.1, s32[32,2]{0,1:T(2,128)S(1)} %copy-done.5), kind=kOutput, calls=%fused_computation.111 | convolution fusion | flops 100925824 | bytes 4723456 | tf_op jit(solution)/shard_map/tcnk,cnb->tbk/dot_general | solution.py:95
  480.8 5.1 %convolution_bitcast_fusion.2 = f32[128,32,2,128]{3,0,2,1:T(8,128)S(1)} fusion(bf16[32,2,128,128]{3,2,1,0:T(8,128)(2,1)S(1)} %copy-done.7, f32[32,128,128,1]{2,1,3,0:T(8,128)S(1)} %copy-done.1), kind=kOutput, calls=%fused_computation.25 | convolution fusion | flops 302514176 | bytes 8388608 | tf_op jit(solution)/shard_map/tck,cnkj->tcnj/dot_general | solution.py:85
  485.9 3.8 fusion.15
  489.8 1.1 fusion.99
  (40 shorter events, 2.1 us)
Async XLA Ops:
  7.2 337.4 %copy-start = (bf16[512,1024]{1,0:T(8,128)(2,1)S(1)}, bf16[512,1024]{1,0:T(8,128)(2,1)}, u32[]{:S(2)}) copy-start(bf16[512,1024]{1,0:T(8,128)(2,1)} %param.21) | copy-start | bytes 3145732
  7.2 147.1 %all-gather.11.cloned.1.call-start = ((), (), s32[]{:S(2)}) async-start(), calls=%async_computation.2 | async-start | bytes 4325376 | tf_op jit(solution)/shard_map/all_gather | solution.py:120
  9.0 306.1 %all-gather.13.cloned.1.call-start = ((), (), s32[]{:S(2)}) async-start(), calls=%async_computation.3 | async-start | bytes 4325376 | tf_op jit(solution)/shard_map/all_gather | solution.py:121
  10.7 390.8 %all-gather.7.cloned.1.call-start = ((), (), s32[]{:S(2)}) async-start(), calls=%async_computation | async-start | bytes 2228224 | tf_op jit(solution)/shard_map/all_gather | solution.py:131
  11.5 455.1 %all-gather.9.cloned.1.call-start = ((), (), s32[]{:S(2)}) async-start(), calls=%async_computation.1 | async-start | bytes 2228224 | tf_op jit(solution)/shard_map/all_gather | solution.py:132
  315.1 29.5 %copy-start.3 = (bf16[1,128,1024]{2,1,0:T(8,128)(2,1)S(1)}, bf16[1,128,1024]{2,1,0:T(8,128)(2,1)}, u32[]{:S(2)}) copy-start(bf16[1,128,1024]{2,1,0:T(8,128)(2,1)} %param.16) | copy-start | bytes 786436
  344.5 0.7 copy-start.4
  466.6 7.2 %copy-start.5 = (s32[32,2]{0,1:T(2,128)S(1)}, s32[32,2]{0,1:T(2,128)}, u32[]{:S(2)}) copy-start(s32[32,2]{0,1:T(2,128)} %param.24) | copy-start | bytes 772
  473.8 7.0 %copy-start.1 = (f32[32,128,128,1]{2,1,3,0:T(8,128)S(1)}, f32[32,128,128,1]{2,1,3,0:T(8,128)}, u32[]{:S(2)}) copy-start(f32[32,128,128,1]{2,1,3,0:T(8,128)} %fusion.32) | copy-start | bytes 6291460
  473.8 7.0 %copy-start.7 = (bf16[32,2,128,128]{3,2,1,0:T(8,128)(2,1)S(1)}, bf16[32,2,128,128]{3,2,1,0:T(8,128)(2,1)}, u32[]{:S(2)}) copy-start(bf16[32,2,128,128]{3,2,1,0:T(8,128)(2,1)} %all-gather.9.cloned.1.call-done) | copy-start | bytes 6291460
  480.8 5.2 %copy-start.6 = (s32[32,2]{0,1:T(2,128)S(1)}, s32[32,2]{0,1:T(2,128)}, u32[]{:S(2)}) copy-start(s32[32,2]{0,1:T(2,128)} %param.26) | copy-start | bytes 772
  485.9 3.8 copy-start.2
Sparse Core Ops, SparseCore 0:
  10.6 143.6 all-gather.10
  156.8 158.1 all-gather.12
  318.4 83.1 all-gather.6
  404.8 61.7 all-gather.8
where the time goes:
time: 498 us; the launch traced here: 497 us
  waiting for transfers between devices  410 us (82%)
  matrix products  53.3 us (11%)
  between operations  13.9 us (3%)
  local copies, waits for them, and re-layouts  10.8 us (2%)
  other arithmetic  8.65 us (2%)
    all_gather x1, waiting for transfers between devices, body(): lax.all_gather(values[0], 'seq', axis=0, tiled=True)  161 us
    all_gather x1, waiting for transfers between devices, body(): lax.all_gather(keys[0], 'seq', axis=0, tiled=True)  134 us
    all_gather x1, waiting for transfers between devices, body(): lax.all_gather(w2_packed, 'grp', axis=0, tiled=True)  60.7 us
    all_gather x1, waiting for transfers between devices, body(): lax.all_gather(w1_packed, 'grp', axis=0, tiled=True)  54 us
    dot_general x8, matrix products, one_head(): return jnp.dot(prob, v_head, preferred_element_type=jnp.float32)  13 us
    dot_general x8, matrix products, one_head(): jnp.dot(q_head, k_head.T, preferred_element_type=jnp.float32) * scale  12.7 us
  transfers between devices with their start and end apart: 4, of which 4 were waited for; matrix products, arithmetic and copies ran while one was open for 9% of the time, Pallas kernels for 0%

commit v1 on v0

--- a/solution.py
+++ b/solution.py
@@ -118,7 +118,9 @@
     allowed = expand_mask(attn_mask[0])
     key_rows, value_rows = (
         lax.all_gather(keys[0], "seq", axis=0, tiled=True),
-        lax.all_gather(values[0], "seq", axis=0, tiled=True),
+        jnp.concatenate(
+            lax.all_to_all(jnp.stack([values[0]] * lax.axis_size("seq")), "seq", 0, 0), axis=0
+        ),
     )
     attn = attend_forward(query, key_rows, value_rows, allowed)
     hidden_state = rows_in.astype(jnp.float32) + jnp.dot(

time: 498 us -> 455 us (0.914)
  waiting for transfers between devices: 410 us -> 339 us
  starting transfers between devices: 0.16 us -> 17.3 us
  local copies, waits for them, and re-layouts: 10.8 us -> 24.6 us
    all_to_all x0 -> x1, waiting for transfers between devices: none -> 194 us  [body(): lax.all_to_all(jnp.stack([values[0]] * lax.axis_size('seq')), 'seq', 0, 0)]
    all_gather x1 -> x0, waiting for transfers between devices: 161 us -> none  [body(): lax.all_gather(values[0], 'seq', axis=0, tiled=True)]
    all_gather x1, waiting for transfers between devices: 134 us -> 40.1 us  [body(): lax.all_gather(keys[0], 'seq', axis=0, tiled=True)]
    all_to_all x0 -> x1, starting transfers between devices: none -> 17.2 us  [body(): lax.all_to_all(jnp.stack([values[0]] * lax.axis_size('seq')), 'seq', 0, 0)]
    another operation x0 -> x3, local copies, waits for them, and re-layouts: none -> 11.4 us  [the longest x1 7.38 us: split_heads(): return array.reshape(array.shape[0], HEADS, HD).transpose(1, 0, 2)]
    all_gather x1, waiting for transfers between devices: 54 us -> 42.7 us  [body(): lax.all_gather(w1_packed, 'grp', axis=0, tiled=True)]
    all_to_all x0 -> x1, local copies, waits for them, and re-layouts: none -> 6.9 us  [body(): lax.all_to_all(jnp.stack([values[0]] * lax.axis_size('seq')), 'seq', 0, 0)]
  transfers between devices with their start and end apart: 4 -> 4, of which waited for: 4 -> 4; matrix products, arithmetic and copies ran while one was open for 9% -> 12% of each run, Pallas kernels for 0% -> 0%
where the time goes in v1:
time: 455 us; the launch traced here: 453 us
  waiting for transfers between devices  339 us (75%)
  matrix products  53.4 us (12%)
  local copies, waits for them, and re-layouts  24.6 us (5%)
  starting transfers between devices  17.3 us (4%)
  between operations  14 us (3%)
  other arithmetic  5.28 us (1%)
    all_to_all x1, waiting for transfers between devices, body(): lax.all_to_all(jnp.stack([values[0]] * lax.axis_size('seq')), 'seq', 0, 0)  194 us
    all_gather x1, waiting for transfers between devices, body(): lax.all_gather(w2_packed, 'grp', axis=0, tiled=True)  60.9 us
    all_gather x1, waiting for transfers between devices, body(): lax.all_gather(w1_packed, 'grp', axis=0, tiled=True)  42.7 us
    all_gather x1, waiting for transfers between devices, body(): lax.all_gather(keys[0], 'seq', axis=0, tiled=True)  40.1 us
    all_to_all x1, starting transfers between devices, body(): lax.all_to_all(jnp.stack([values[0]] * lax.axis_size('seq')), 'seq', 0, 0)  17.2 us
    dot_general x8, matrix products, one_head(): return jnp.dot(prob, v_head, preferred_element_type=jnp.float32)  13 us
    dot_general x8, matrix products, one_head(): jnp.dot(q_head, k_head.T, preferred_element_type=jnp.float32) * scale  12.7 us
  transfers between devices with their start and end apart: 4, of which 4 were waited for; matrix products, arithmetic and copies ran while one was open for 12% of the time, Pallas kernels for 0%

profile of v1, /device:TPU:1, one launch (start us, length us, event | category | flops | bytes accessed | tf_op | source)
XLA Modules:
  0.0 453.4 jit_solution(1834974135162687152)
XLA Ops:
  7.2 1.1 copy.47
  8.3 2.9 stack.3
  11.2 17.2 %all-to-all-start = ((bf16[32,128,512]{1,2,0:T(8,128)(2,1)}), bf16[32,128,512]{1,2,0:T(8,128)(2,1)}, u32[]{:S(2)}, u32[]{:S(2)}) async-start(bf16[32,128,512]{1,2,0:T(8,128)(2,1)} %stack.3), calls=%async_computation | async-start | bytes 8388608 | tf_op jit(solution)/shard_map/all_to_all | solution.py:122
  28.5 0.8 copy.46
  29.4 0.7 all-gather.5.cloned.1.call-update
  30.1 0.7 all-gather.7.cloned.1.call-update
  32.0 2.1 gather_fusion.1
  34.2 193.7 %all-to-all-done = bf16[32,128,512]{1,2,0:T(8,128)(2,1)} async-done(((bf16[32,128,512]{1,2,0:T(8,128)(2,1)}), bf16[32,128,512]{1,2,0:T(8,128)(2,1)}, u32[]{:S(2)}, u32[]{:S(2)}) %all-to-all-start) | async-done | bytes 4194336 | tf_op jit(solution)/shard_map/all_to_all | solution.py:122
  227.9 6.9 %copy.48 = bf16[32,128,512]{1,0,2:T(8,128)(2,1)} copy(bf16[32,128,512]{1,2,0:T(8,128)(2,1)} %all-to-all-done) | data formatting | bytes 8388608 | tf_op jit(solution)/shard_map/all_to_all | solution.py:122
  234.8 7.4 %reshape_reshape.3 = bf16[4096,8,64]{0,2,1:T(8,128)(2,1)} reshape(bf16[32,128,512]{1,0,2:T(8,128)(2,1)} %copy.48) | data formatting | bytes 8388608 | tf_op jit(solution)/shard_map/reshape;reshape | solution.py:26
  242.2 40.1 %all-gather.9.cloned.1.call-done = bf16[1,4096,512]{1,2,0:T(8,128)(2,1)} async-done(((bf16[1,128,512]{1,2,0:T(8,128)(2,1)}), bf16[1,4096,512]{1,2,0:T(8,128)(2,1)}) %all-gather.9.cloned.1.call-update) | async-done | bytes 4194320 | tf_op jit(solution)/shard_map/all_gather | solution.py:120
  282.3 29.5 %while.11 = (s32[]{:T(128)}, bf16[8,128,64]{1,2,0:T(8,128)(2,1)S(1)}, bf16[8,128,64]{1,2,0:T(8,128)(2,1)S(1)}, bf16[8,4096,64]{1,2,0:T(8,128)(2,1)}, bf16[8,4096...) while((s32[]{:T(128)}, bf16[8,128,64]{1,2,0:T(8,128)(2,1)S(1)}, ...), condition=%wide.region_3.4_spmd.clone, body=%wide.region_0.3_spmd.clone.sunk | while | flops 138411776 | bytes 7397965 | solution.py:46
  282.3 1.6 fusion.158
  283.9 0.4 fusion.159
  284.4 1.6 fusion.160
  286.0 1.6 fusion.158
  287.6 0.4 fusion.159
  288.0 1.6 fusion.160
  289.7 1.6 fusion.158
  291.3 0.4 fusion.159
  291.7 1.6 fusion.160
  293.4 1.6 fusion.158
  294.9 0.4 fusion.159
  295.4 1.6 fusion.160
  297.0 1.6 fusion.158
  298.6 0.4 fusion.159
  299.1 1.6 fusion.160
  300.7 1.6 fusion.158
  302.3 0.4 fusion.159
  302.8 1.6 fusion.160
  304.4 1.6 fusion.158
  306.0 0.4 fusion.159
  306.4 1.6 fusion.160
  308.1 1.6 fusion.158
  309.7 0.4 fusion.159
  310.1 1.6 fusion.160
  311.8 0.4 fusion.145
  312.2 0.2 multiply_reduce_fusion.1
  312.6 2.1 gather_fusion
  314.8 42.7 %all-gather.5.cloned.1.call-done = bf16[32,2,128,128]{3,2,1,0:T(8,128)(2,1)} async-done(((bf16[2,2,128,128]{3,2,1,0:T(8,128)(2,1)}), bf16[32,2,128,128]{3,2,1,0:T(8,128)(2,1)}) %all-gather.5.cloned.1.call-update) | async-done | bytes 2097168 | tf_op jit(solution)/shard_map/all_gather | solution.py:133
  357.4 4.3 fusion.32
  361.8 60.9 %all-gather.7.cloned.1.call-done = bf16[32,2,128,128]{3,2,1,0:T(8,128)(2,1)} async-done(((bf16[2,2,128,128]{3,2,1,0:T(8,128)(2,1)}), bf16[32,2,128,128]{3,2,1,0:T(8,128)(2,1)}) %all-gather.7.cloned.1.call-update) | async-done | bytes 2097168 | tf_op jit(solution)/shard_map/all_gather | solution.py:134
  422.6 7.2 %convolution_bitcast_fusion.1 = f32[128,32,2,128]{3,0,2,1:T(8,128)} fusion(bf16[32,2,128,128]{3,2,1,0:T(8,128)(2,1)} %all-gather.5.cloned.1.call-done, f32[32,128,128,1]{2,1,3,0:T(8,128)} %fusion.32, bf16[32,2,128,128]{3,2,1,0:T(8,128)(2,1)} %all-gather.7.cloned.1.call-done, bf16[32,2,128,128]{3,2,1,0:T(8,128)(2,1)} %bitcast.204, pred[32,2]{1,0:T(8,128)(4,1)S(1)} %copy.56), kind=kOutput, calls=%fused_computation.24 | convolution fusion | flops 543162368 | bytes 12582976 | tf_op jit(solution)/shard_map/tcj,cnkj->tcnk/dot_general | solution.py:94
  429.8 6.7 %fusion.96 = (f32[128]{0:T(128)S(1)}, f32[8,128,128,1]{2,0,3,1:T(8,128)S(1)}) fusion(f32[8,128]{1,0:T(8,128)S(1)} %bitcast.211, f32[128,32,2,128]{3,0,2,1:T(8,128)} %convolution_bitcast_fusion.1, s32[32,2]{0,1:T(2,128)S(1)} %copy-done.7), kind=kOutput, calls=%fused_computation.111 | convolution fusion | flops 100925824 | bytes 4723456 | tf_op jit(solution)/shard_map/tcnk,cnb->tbk/dot_general | solution.py:95
  436.5 0.2 multiply_reduce_fusion
  436.8 5.2 %convolution_bitcast_fusion.2 = f32[128,32,2,128]{3,0,2,1:T(8,128)S(1)} fusion(bf16[32,2,128,128]{3,2,1,0:T(8,128)(2,1)S(1)} %copy-done.9, f32[32,128,128,1]{2,1,3,0:T(8,128)S(1)} %copy-done.1), kind=kOutput, calls=%fused_computation.25 | convolution fusion | flops 302514176 | bytes 8388608 | tf_op jit(solution)/shard_map/tck,cnkj->tcnj/dot_general | solution.py:85
  441.9 3.8 fusion.15
  445.8 1.1 fusion.99
  (48 shorter events, 1.6 us)
Async XLA Ops:
  7.2 304.6 %copy-start = (bf16[512,1024]{1,0:T(8,128)(2,1)S(1)}, bf16[512,1024]{1,0:T(8,128)(2,1)}, u32[]{:S(2)}) copy-start(bf16[512,1024]{1,0:T(8,128)(2,1)} %param.21) | copy-start | bytes 3145732
  11.2 17.3 %copy-start.4 = (bf16[1,128,512]{2,1,0:T(8,128)(2,1)S(1)}, bf16[1,128,512]{2,1,0:T(8,128)(2,1)}, u32[]{:S(2)}) copy-start(bf16[1,128,512]{2,1,0:T(8,128)(2,1)} %param.18) | copy-start | bytes 393220
  11.2 19.6 %copy-start.5 = (bf16[1,128,512]{2,1,0:T(8,128)(2,1)S(1)}, bf16[1,128,512]{2,1,0:T(8,128)(2,1)}, u32[]{:S(2)}) copy-start(bf16[1,128,512]{2,1,0:T(8,128)(2,1)} %param.17) | copy-start | bytes 393220
  11.2 19.7 %copy-start.7 = (s32[32,2]{0,1:T(2,128)S(1)}, s32[32,2]{0,1:T(2,128)}, u32[]{:S(2)}) copy-start(s32[32,2]{0,1:T(2,128)} %param.24) | copy-start | bytes 772
  11.2 20.1 %copy-start.2 = (bf16[1,128,1024]{2,1,0:T(8,128)(2,1)S(1)}, bf16[1,128,1024]{2,1,0:T(8,128)(2,1)}, u32[]{:S(2)}) copy-start(bf16[1,128,1024]{2,1,0:T(8,128)(2,1)} %param.27) | copy-start | bytes 786436
  11.2 20.4 %copy-start.8 = (s32[32,2]{0,1:T(2,128)S(1)}, s32[32,2]{0,1:T(2,128)}, u32[]{:S(2)}) copy-start(s32[32,2]{0,1:T(2,128)} %param.26) | copy-start | bytes 772
  11.2 216.7 %all-to-all-start = ((bf16[32,128,512]{1,2,0:T(8,128)(2,1)}), bf16[32,128,512]{1,2,0:T(8,128)(2,1)}, u32[]{:S(2)}, u32[]{:S(2)}) async-start(bf16[32,128,512]{1,2,0:T(8,128)(2,1)} %stack.3), calls=%async_computation | async-start | bytes 8388608 | tf_op jit(solution)/shard_map/all_to_all | solution.py:122
  28.5 253.8 %all-gather.9.cloned.1.call-start = ((), (), s32[]{:S(2)}) async-start(), calls=%async_computation.3 | async-start | bytes 4325376 | tf_op jit(solution)/shard_map/all_gather | solution.py:120
  29.3 328.1 %all-gather.5.cloned.1.call-start = ((), (), s32[]{:S(2)}) async-start(), calls=%async_computation.1 | async-start | bytes 2228224 | tf_op jit(solution)/shard_map/all_gather | solution.py:133
  30.1 392.6 %all-gather.7.cloned.1.call-start = ((), (), s32[]{:S(2)}) async-start(), calls=%async_computation.2 | async-start | bytes 2228224 | tf_op jit(solution)/shard_map/all_gather | solution.py:134
  32.0 2.2 copy-start.10
  282.3 29.5 %copy-start.3 = (bf16[1,128,1024]{2,1,0:T(8,128)(2,1)S(1)}, bf16[1,128,1024]{2,1,0:T(8,128)(2,1)}, u32[]{:S(2)}) copy-start(bf16[1,128,1024]{2,1,0:T(8,128)(2,1)} %param.16) | copy-start | bytes 786436
  311.8 0.7 copy-start.6
  429.8 7.0 %copy-start.1 = (f32[32,128,128,1]{2,1,3,0:T(8,128)S(1)}, f32[32,128,128,1]{2,1,3,0:T(8,128)}, u32[]{:S(2)}) copy-start(f32[32,128,128,1]{2,1,3,0:T(8,128)} %fusion.32) | copy-start | bytes 6291460
  429.8 7.0 %copy-start.9 = (bf16[32,2,128,128]{3,2,1,0:T(8,128)(2,1)S(1)}, bf16[32,2,128,128]{3,2,1,0:T(8,128)(2,1)}, u32[]{:S(2)}) copy-start(bf16[32,2,128,128]{3,2,1,0:T(8,128)(2,1)} %all-gather.7.cloned.1.call-done) | copy-start | bytes 6291460
Sparse Core Ops, SparseCore 0:
  31.9 250.3 all-gather.8
  285.6 71.7 all-gather.4
  360.8 61.7 all-gather.6
